TPU v7x, 32 devices: a whole 2x2x4 slice. The times are simulated.
32 devices in a mesh: groups: 2 (over x), gx: 16 (over z, y, core).
Axes of the slice: x: 2, y: 2, z: 4, core: 2. Of those that a mesh axis runs over, the one named last changes fastest.
Arguments:
- features: bfloat16 [64, 16, 64, 128], P(('groups', 'gx')), parts along dimension 0, may hold values from -6 to 6
- cotangent: bfloat16 [64, 16, 64, 128], P(('groups', 'gx')), parts along dimension 0, may hold values from -6 to 6
- wall_flags: int32 [64, 16, 128], P(('groups', 'gx')), parts along dimension 0, may hold values 0 or 1
- mode_counts: int32 [64], replicated, may hold values from 1 to 16, as said below
- offsets: int32 [6, 3], replicated, may hold values from -2 to 2, as said below
- point_weight: bfloat16 [64, 64], replicated, may hold values from -0.75 to 0.75
- kernel_weight: bfloat16 [6, 64, 64], replicated, may hold values from -0.3125 to 0.3125
- lap_weight: bfloat16 [64, 64], replicated, may hold values from -0.125 to 0.125
- spec_weight: bfloat16 [16, 64, 64], replicated, may hold values from -1 to 1
- bias: float32 [64], replicated, may hold values from -3 to 3
Outputs:
- input_grad: bfloat16 [64, 16, 64, 128], P(('groups', 'gx')), parts along dimension 0
- kernel_grad: float32 [12, 64, 64], P('groups'), parts along dimension 0
There are 2 independent parts, one for each index of `groups`. A program takes and returns all parts, laid end to end along the dimension named above; an argument that names none is the same for every part. Nothing has to cross between parts.
Inputs may be any that keep to these rules, and one draw needn't show every extreme that they name: Column 0 holds x offsets in -1..1 and both -1 and 1 occur; columns 1 and 2 hold y and z offsets in -2..2, and -2 and 2 occur in each of them. `mode_counts`: some channel keeps 16 modes and some channel keeps 1.
All inputs are finite; a program needn't handle non-finite values. No bound on the sum of `wall_flags` on one device may be relied on, other than what follows from the above.
Results may differ from a plain program's by a relative error of at most 0.0066.
Values may be sent and summed in bfloat16 or wider, within the bound.
A program may use at most 256 MiB of HBM per device.

v0:
```python
from functools import partial
import math
import jax
import jax.numpy as jnp
from jax import lax
from jax.sharding import PartitionSpec as P

RAD = 2


def with_halo(cells, sides, width):
    for axis, dim in sides:
        count = lax.axis_size(axis)
        ends = count - 1
        head = lax.slice_in_dim(cells, 0, width, axis=dim)
        tail = lax.slice_in_dim(cells, cells.shape[dim] - width, cells.shape[dim], axis=dim)
        cells = jnp.concatenate(
            [
                lax.ppermute(tail, axis, [(i, (i + 1) % count) for i in range(ends)]),
                cells,
                lax.ppermute(head, axis, [((i + 1) % count, i) for i in range(ends)]),
            ],
            axis=dim,
        )
    return cells


def basis_table(mode_total, length):
    mode_index = jnp.arange(mode_total, dtype=jnp.float32)[:, None]
    cell_index = jnp.arange(length, dtype=jnp.float32)[None, :]
    phase_angle = math.pi / (2.0 * length) * mode_index * (2.0 * cell_index + 1.0)
    amplitude = jnp.where(mode_index == 0.0, math.sqrt(1.0 / length), math.sqrt(2.0 / length))
    return (amplitude * jnp.cos(phase_angle)).astype(jnp.bfloat16)


def pencil_work(pencil, spec_weight, kept_modes, adjoint):
    basis = basis_table(spec_weight.shape[0], pencil.shape[0])
    coefficients = jnp.einsum(
        "kx,xycz->kycz", basis, pencil, preferred_element_type=jnp.float32
    ).astype(jnp.bfloat16)
    if adjoint:
        masked = coefficients * kept_modes[:, None, :, None].astype(jnp.bfloat16)
        mixed_modes = jnp.einsum(
            "koc,kyoz->kycz", spec_weight, masked, preferred_element_type=jnp.float32
        ).astype(jnp.bfloat16)
    else:
        mixed_modes = jnp.einsum(
            "koc,kycz->kyoz", spec_weight, coefficients, preferred_element_type=jnp.float32
        )
        mixed_modes = (mixed_modes * kept_modes[:, None, :, None]).astype(jnp.bfloat16)
    return jnp.einsum(
        "kx,kyoz->xyoz", basis, mixed_modes, preferred_element_type=jnp.float32
    ).astype(jnp.bfloat16)


def spectral(slab, spec_weight, kept_modes, adjoint):
    result = pencil_work(
        lax.all_to_all(slab, "gx", split_axis=1, concat_axis=0, tiled=True),
        spec_weight,
        kept_modes,
        adjoint,
    )
    return lax.all_to_all(result, "gx", split_axis=0, concat_axis=1, tiled=True)


def laplace_ext(extended):
    padded = jnp.pad(extended, ((0, 0), (1, 1), (0, 0), (1, 1))).astype(jnp.float32)
    centre_cells = padded[1:-1, 1:-1, :, 1:-1]
    neighbours = padded[2:, 1:-1, :, 1:-1] + padded[:-2, 1:-1, :, 1:-1]
    neighbours = neighbours + padded[1:-1, 2:, :, 1:-1] + padded[1:-1, :-2, :, 1:-1]
    neighbours = neighbours + padded[1:-1, 1:-1, :, 2:] + padded[1:-1, 1:-1, :, :-2]
    return (neighbours - 6.0 * centre_cells).astype(jnp.bfloat16)


def pad_sides(extended):
    return jnp.pad(extended, ((0, 0), (RAD, RAD), (0, 0), (RAD, RAD)))


def window_of(padded, offset, direction, slab_shape):
    starts = (
        1 + direction * offset[0],
        RAD + direction * offset[1],
        0,
        RAD + direction * offset[2],
    )
    return lax.dynamic_slice(padded, starts, slab_shape)


def gelu_slope(preact, upstream):
    _, pullback = jax.vjp(partial(jax.nn.gelu, approximate=True), preact)
    return pullback(upstream)[0]


def per_device(
    features,
    cotangent,
    wall_flags,
    mode_counts,
    offsets,
    point_weight,
    kernel_weight,
    lap_weight,
    spec_weight,
    bias,
):
    mode_total = spec_weight.shape[0]
    tile_total = kernel_weight.shape[0]
    kept_modes = (jnp.arange(mode_total, dtype=jnp.int32)[:, None] < mode_counts[None, :]).astype(
        jnp.float32
    )
    fluid_mask = (1 - wall_flags).astype(jnp.float32)[:, :, None, :]
    extended = with_halo(features, (("gx", 0),), 1)
    padded_field = pad_sides(extended)
    local_part = jnp.einsum(
        "oc,xycz->xyoz", point_weight, features, preferred_element_type=jnp.float32
    )
    local_part = local_part + jnp.einsum(
        "oc,xycz->xyoz", lap_weight, laplace_ext(extended), preferred_element_type=jnp.float32
    )
    for tile in range(tile_total):
        moved = window_of(padded_field, offsets[tile], 1, features.shape)
        local_part = local_part + jnp.einsum(
            "oc,xycz->xyoz", kernel_weight[tile], moved, preferred_element_type=jnp.float32
        )
    local_part = local_part + bias[:, None]
    spectral_part = spectral(features, spec_weight, kept_modes, False)
    preact = local_part + spectral_part.astype(jnp.float32)
    weighted = (gelu_slope(preact, cotangent.astype(jnp.float32)) * fluid_mask).astype(jnp.bfloat16)
    spec_grad = spectral(weighted, spec_weight, kept_modes, True)
    ext_grad = with_halo(weighted, (("gx", 0),), 1)
    padded_grad = pad_sides(ext_grad)
    input_grad = jnp.einsum(
        "oc,xyoz->xycz", point_weight, weighted, preferred_element_type=jnp.float32
    )
    input_grad = input_grad + jnp.einsum(
        "oc,xyoz->xycz", lap_weight, laplace_ext(ext_grad), preferred_element_type=jnp.float32
    )
    input_grad = input_grad + spec_grad.astype(jnp.float32)
    tile_grads = []
    for tile in range(tile_total):
        back_moved = window_of(padded_grad, offsets[tile], -1, weighted.shape)
        input_grad = input_grad + jnp.einsum(
            "oc,xyoz->xycz", kernel_weight[tile], back_moved, preferred_element_type=jnp.float32
        )
        tile_grads.append(
            jnp.einsum("xyoz,xycz->oc", back_moved, features, preferred_element_type=jnp.float32)
        )
    local_grad = jnp.stack(tile_grads, axis=0)
    scaling = float(
        lax.axis_size("gx") * features.shape[0] * features.shape[1] * features.shape[3]
    ) ** (-0.5)
    summed = lax.psum(local_grad, "gx")
    return (input_grad.astype(jnp.bfloat16), summed * scaling)


def solution(mesh):
    return jax.shard_map(
        per_device,
        mesh=mesh,
        in_specs=(
            P(("groups", "gx"), None, None, None),
            P(("groups", "gx"), None, None, None),
            P(("groups", "gx"), None, None),
            P(),
            P(),
            P(),
            P(),
            P(),
            P(),
            P(),
        ),
        out_specs=(P(("groups", "gx"), None, None, None), P("groups", None, None)),
        check_vma=False,
    )
```

profile of v0, /device:TPU:0, one launch (start us, length us, event | category | flops | bytes accessed | tf_op | source)
XLA Modules:
  0.0 241.2 jit_solution(13705008029308537028)
XLA Ops:
  7.2 1.1 fusion.148
  8.4 2.4 collective-permute-start
  10.7 1.3 collective-permute-start.1
  12.0 1.9 copy.40
  13.9 9.4 %all-to-all-start = ((bf16[2,16,64,128]{3,2,0,1:T(8,128)(2,1)}), bf16[2,16,64,128]{3,2,0,1:T(8,128)(2,1)S(1)}, u32[]{:S(2)}, u32[]{:S(2)}) async-start(bf16[2,16,64,128]{3,2,0,1:T(8,128)(2,1)} %copy.40), calls=%async_computation | async-start | bytes 1048576 | tf_op jit(solution)/shard_map/all_to_all | solution.py:58
  23.4 1.3 fusion.76
  61.1 1.5 fusion.48
  62.6 1.4 fusion.49
  64.0 1.1 convolution_convert_fusion.4
  65.3 1.1 fusion.17
  67.4 6.0 %all-to-all-start.1 = ((bf16[32,1,64,128]{3,2,1,0:T(8,128)(2,1)}), bf16[32,1,64,128]{3,2,1,0:T(8,128)(2,1)S(1)}, u32[]{:S(2)}, u32[]{:S(2)}) async-start(bf16[32,1,64,128]{3,2,1,0:T(8,128)(2,1)} %copy.44), calls=%async_computation.1 | async-start | bytes 1048576 | tf_op jit(solution)/shard_map/all_to_all | solution.py:63
  74.2 1.4 fusion.50
  75.7 1.4 fusion.51
  77.1 2.9 %convolution_add_fusion.1 = f32[2,16,128,64]{2,3,1,0:T(8,128)} fusion(f32[2,16,128,64]{2,3,1,0:T(8,128)S(1)} %copy-done.3, f32[4,18,64,130]{3,2,1,0:T(8,128)S(1)} %pad_convert_fusion.1, bf16[64,64]{1,0:T(8,128)(2,1)S(1)} %copy-done.12), kind=kOutput, calls=%fused_computation.37 | convolution fusion | flops 35913728 | bytes 9453568 | tf_op jit(solution)/shard_map/oc,xycz->xyoz/dot_general | solution.py:117
  79.9 8.0 %all-to-all-done.1 = bf16[32,1,64,128]{3,2,1,0:T(8,128)(2,1)S(1)} async-done(((bf16[32,1,64,128]{3,2,1,0:T(8,128)(2,1)}), bf16[32,1,64,128]{3,2,1,0:T(8,128)(2,1)S(1)}, u32[]{:S(2)}, u32[]{:S(2)}) %all-to-all-start.1) | async-done | bytes 524320 | tf_op jit(solution)/shard_map/all_to_all | solution.py:63
  88.7 4.2 %fusion.33 = bf16[2,16,64,128]{3,2,1,0:T(8,128)(2,1)S(1)} fusion(bf16[2,16,64,128]{3,2,1,0:T(8,128)(2,1)} %param.11, f32[2,16,128,64]{2,3,1,0:T(8,128)} %fusion.51, f32[2,16,128,64]{2,3,1,0:T(8,128)} %fusion.50, f32[2,16,128,64]{2,3,1,0:T(8,128)} %fusion.49, f32[2,16,128,64]{2,3,1,0:T(8,128)} %fusion.48, f32[2,16,128,64]{2,3,1,0:T(8,128)S(1)} %fusion.47, ...), kind=kOutput, calls=%fused_computation.72 | convolution fusion | flops 41680896 | bytes 8946188 | tf_op jit(solution)/shard_map/oc,xycz->xyoz/dot_general | solution.py:122
  93.7 1.9 collective-permute-start.2
  95.7 1.3 collective-permute-start.3
  97.0 6.9 %all-to-all-start.2 = ((bf16[2,16,64,128]{3,2,0,1:T(8,128)(2,1)}), bf16[2,16,64,128]{3,2,0,1:T(8,128)(2,1)}, u32[]{:S(2)}, u32[]{:S(2)}) async-start(bf16[2,16,64,128]{3,2,0,1:T(8,128)(2,1)} %copy.49), calls=%async_computation.2 | async-start | bytes 1048576 | tf_op jit(solution)/shard_map/all_to_all | solution.py:58
  103.9 1.3 fusion.74
  110.9 1.5 convolution_bitcast_fusion.2
  112.3 1.4 convolution_bitcast_fusion.3
  113.7 4.7 %all-to-all-done.2 = bf16[2,16,64,128]{3,2,0,1:T(8,128)(2,1)} async-done(((bf16[2,16,64,128]{3,2,0,1:T(8,128)(2,1)}), bf16[2,16,64,128]{3,2,0,1:T(8,128)(2,1)}, u32[]{:S(2)}, u32[]{:S(2)}) %all-to-all-start.2) | async-done | bytes 524320 | tf_op jit(solution)/shard_map/all_to_all | solution.py:58
  118.4 1.5 fusion.22
  121.7 4.1 %all-to-all-start.3 = ((bf16[32,1,64,128]{3,2,1,0:T(8,128)(2,1)}), bf16[32,1,64,128]{3,2,1,0:T(8,128)(2,1)S(1)}, u32[]{:S(2)}, u32[]{:S(2)}) async-start(bf16[32,1,64,128]{3,2,1,0:T(8,128)(2,1)} %copy.55), calls=%async_computation.3 | async-start | bytes 1048576 | tf_op jit(solution)/shard_map/all_to_all | solution.py:63
  126.9 1.4 convolution_bitcast_fusion.4
  128.3 1.5 convolution_bitcast_fusion
  129.8 2.9 %pad_convert_fusion = f32[4,18,64,130]{3,2,1,0:T(8,128)} fusion(bf16[4,16,64,128]{3,2,1,0:T(8,128)(2,1)S(1)} %pad_maximum_fusion), kind=kLoop, calls=%fused_computation.12 | loop fusion | flops 599040 | bytes 3444736 | tf_op jit(solution)/shard_map/convert_element_type | solution.py:67
  132.7 89.0 %all-reduce.6.cloned.1.call-done = f32[6,64,64]{2,1,0:T(8,128)} async-done(((f32[6,64,64]{2,1,0:T(8,128)}), f32[6,64,64]{2,1,0:T(8,128)}) %all-reduce.6.cloned.1.call-update) | async-done | bytes 98320 | tf_op jit(solution)/shard_map/psum | solution.py:152
  221.7 1.6 broadcast_multiply_fusion
  223.4 7.5 %fusion.15 = f32[2,16,64,128]{3,2,1,0:T(8,128)S(1)} fusion(f32[2,16,128,64]{2,3,1,0:T(8,128)} %fusion.74, f32[4,18,64,130]{3,2,1,0:T(8,128)} %pad_convert_fusion, bf16[64,64]{1,0:T(8,128)(2,1)S(1)} %copy-done.13, bf16[16,2,1,64,128]{4,3,1,0,2:T(8,128)(2,1)S(1)} %bitcast.306), kind=kOutput, calls=%fused_computation.40 | convolution fusion | flops 36438016 | bytes 9969664 | tf_op jit(solution)/shard_map/oc,xyoz->xycz/dot_general | solution.py:135
  230.8 3.5 %fusion.16 = bf16[2,16,64,128]{3,2,1,0:T(8,128)(2,1)} fusion(f32[2,16,64,128]{3,2,1,0:T(8,128)} %convolution_bitcast_fusion, f32[2,16,64,128]{3,2,1,0:T(8,128)S(1)} %convolution_bitcast_fusion.1, f32[2,16,64,128]{3,2,1,0:T(8,128)} %convolution_bitcast_fusion.2, f32[2,16,64,128]{3,2,1,0:T(8,128)} %convolution_bitcast_fusion.3, ...), kind=kOutput, calls=%fused_computation.43 | convolution fusion | flops 35389440 | bytes 7880716 | tf_op jit(solution)/shard_map/oc,xyoz->xycz/dot_general | solution.py:142
  (62 shorter events, 14.6 us)
Async XLA Ops:
  7.2 57.9 %copy-start = (bf16[16,64,64]{2,1,0:T(8,128)(2,1)S(1)}, bf16[16,64,64]{2,1,0:T(8,128)(2,1)}, u32[]{:S(2)}) copy-start(bf16[16,64,64]{2,1,0:T(8,128)(2,1)} %param.18) | copy-start | bytes 393220
  7.2 16.2 %copy-start.1 = (bf16[2,16,64,128]{3,2,1,0:T(8,128)(2,1)S(1)}, bf16[2,16,64,128]{3,2,1,0:T(8,128)(2,1)}, u32[]{:S(2)}) copy-start(bf16[2,16,64,128]{3,2,1,0:T(8,128)(2,1)} %param.10) | copy-start | bytes 1572868
  7.2 16.2 %copy-start.11 = (s32[64]{0:T(128)S(1)}, s32[64]{0:T(128)}, u32[]{:S(2)}) copy-start(s32[64]{0:T(128)} %param.13) | copy-start | bytes 772
  7.2 16.2 %copy-start.5 = (bf16[64,64]{1,0:T(8,128)(2,1)S(1)}, bf16[64,64]{1,0:T(8,128)(2,1)}, u32[]{:S(2)}) copy-start(bf16[64,64]{1,0:T(8,128)(2,1)} %param.15) | copy-start | bytes 24580
  7.2 17.5 %copy-start.8 = (s32[2,16,128]{2,1,0:T(8,128)S(1)}, s32[2,16,128]{2,1,0:T(8,128)}, u32[]{:S(2)}) copy-start(s32[2,16,128]{2,1,0:T(8,128)} %param.12) | copy-start | bytes 49156
  7.2 17.5 %copy-start.6 = (s32[6,3]{0,1:T(4,128)S(1)}, s32[6,3]{0,1:T(4,128)}, u32[]{:S(2)}) copy-start(s32[6,3]{0,1:T(4,128)} %param.14) | copy-start | bytes 220
  8.4 52.2 %collective-permute-start = (bf16[1,16,64,128]{3,2,1,0:T(8,128)(2,1)S(1)}, bf16[1,16,64,128]{3,2,1,0:T(8,128)(2,1)S(1)}, u32[]{:S(2)}, u32[]{:S(2)}) collective-permute-start(bf16[1,16,64,128]{3,2,1,0:T(8,128)(2,1)S(1)} %get-tuple-element.5), channel_id=1, source_target_pairs={{0,1},{1,2},{2,3},{3,4},{4,5},{5,6},{6,7},{7,8},{8,9},{9,10},{10,1... | collective-permute-start | bytes 786440 | tf_op jit(solution)/shard_map/ppermute | solution.py:19
  10.7 49.9 %collective-permute-start.1 = (bf16[1,16,64,128]{3,2,1,0:T(8,128)(2,1)S(1)}, bf16[1,16,64,128]{3,2,1,0:T(8,128)(2,1)S(1)}, u32[]{:S(2)}, u32[]{:S(2)}) collective-permute-start(bf16[1,16,64,128]{3,2,1,0:T(8,128)(2,1)S(1)} %get-tuple-element.4), channel_id=1, source_target_pairs={{1,0},{2,1},{3,2},{4,3},{5,4},{6,5},{7,6},{8,7},{9,8},{10,9},{11,1... | collective-permute-start | bytes 786440 | tf_op jit(solution)/shard_map/ppermute | solution.py:21
  13.9 46.8 %copy-start.4 = (bf16[6,64,64]{2,1,0:T(8,128)(2,1)S(1)}, bf16[6,64,64]{2,1,0:T(8,128)(2,1)}, u32[]{:S(2)}) copy-start(bf16[6,64,64]{2,1,0:T(8,128)(2,1)} %param.16) | copy-start | bytes 147460
  13.9 50.1 %all-to-all-start = ((bf16[2,16,64,128]{3,2,0,1:T(8,128)(2,1)}), bf16[2,16,64,128]{3,2,0,1:T(8,128)(2,1)S(1)}, u32[]{:S(2)}, u32[]{:S(2)}) async-start(bf16[2,16,64,128]{3,2,0,1:T(8,128)(2,1)} %copy.40), calls=%async_computation | async-start | bytes 1048576 | tf_op jit(solution)/shard_map/all_to_all | solution.py:58
  67.4 20.5 %all-to-all-start.1 = ((bf16[32,1,64,128]{3,2,1,0:T(8,128)(2,1)}), bf16[32,1,64,128]{3,2,1,0:T(8,128)(2,1)S(1)}, u32[]{:S(2)}, u32[]{:S(2)}) async-start(bf16[32,1,64,128]{3,2,1,0:T(8,128)(2,1)} %copy.44), calls=%async_computation.1 | async-start | bytes 1048576 | tf_op jit(solution)/shard_map/all_to_all | solution.py:63
  74.2 2.9 %copy-start.3 = (f32[2,16,128,64]{2,3,1,0:T(8,128)S(1)}, f32[2,16,128,64]{2,3,1,0:T(8,128)}, u32[]{:S(2)}) copy-start(f32[2,16,128,64]{2,3,1,0:T(8,128)} %fusion.76) | copy-start | bytes 3145732
  74.2 2.9 %copy-start.12 = (bf16[64,64]{1,0:T(8,128)(2,1)S(1)}, bf16[64,64]{1,0:T(8,128)(2,1)}, u32[]{:S(2)}) copy-start(bf16[64,64]{1,0:T(8,128)(2,1)} %param.17) | copy-start | bytes 24580
  75.7 13.0 %copy-start.10 = (f32[64]{0:T(128)S(1)}, f32[64]{0:T(128)}, u32[]{:S(2)}) copy-start(f32[64]{0:T(128)} %param.19) | copy-start | bytes 772
  87.9 0.8 copy-start.2
  93.7 11.5 %collective-permute-start.2 = (bf16[1,16,64,128]{3,2,1,0:T(8,128)(2,1)S(1)}, bf16[1,16,64,128]{3,2,1,0:T(8,128)(2,1)S(1)}, u32[]{:S(2)}, u32[]{:S(2)}) collective-permute-start(bf16[1,16,64,128]{3,2,1,0:T(8,128)(2,1)S(1)} %get-tuple-element.2), channel_id=1, source_target_pairs={{0,1},{1,2},{2,3},{3,4},{4,5},{5,6},{6,7},{7,8},{8,9},{9,10},{10,1... | collective-permute-start | bytes 786440 | tf_op jit(solution)/shard_map/ppermute | solution.py:19
  95.7 9.6 %collective-permute-start.3 = (bf16[1,16,64,128]{3,2,1,0:T(8,128)(2,1)S(1)}, bf16[1,16,64,128]{3,2,1,0:T(8,128)(2,1)S(1)}, u32[]{:S(2)}, u32[]{:S(2)}) collective-permute-start(bf16[1,16,64,128]{3,2,1,0:T(8,128)(2,1)S(1)} %get-tuple-element.3), channel_id=1, source_target_pairs={{1,0},{2,1},{3,2},{4,3},{5,4},{6,5},{7,6},{8,7},{9,8},{10,9},{11,1... | collective-permute-start | bytes 786440 | tf_op jit(solution)/shard_map/ppermute | solution.py:21
  97.0 21.5 %all-to-all-start.2 = ((bf16[2,16,64,128]{3,2,0,1:T(8,128)(2,1)}), bf16[2,16,64,128]{3,2,0,1:T(8,128)(2,1)}, u32[]{:S(2)}, u32[]{:S(2)}) async-start(bf16[2,16,64,128]{3,2,0,1:T(8,128)(2,1)} %copy.49), calls=%async_computation.2 | async-start | bytes 1048576 | tf_op jit(solution)/shard_map/all_to_all | solution.py:58
  110.8 7.6 %copy-start.7 = (bf16[16,64]{0,1:T(8,128)(2,1)S(1)}, bf16[16,64]{0,1:T(8,128)(2,1)}, u32[]{:S(2)}) copy-start(bf16[16,64]{0,1:T(8,128)(2,1)} %copy.51) | copy-start | bytes 6148
  110.8 7.6 %copy-start.9 = (f32[32]{0:T(128)S(1)}, f32[32]{0:T(128)}, u32[]{:S(2)}) copy-start(f32[32]{0:T(128)} %multiply_add_fusion) | copy-start | bytes 388
  121.7 101.7 %all-to-all-start.3 = ((bf16[32,1,64,128]{3,2,1,0:T(8,128)(2,1)}), bf16[32,1,64,128]{3,2,1,0:T(8,128)(2,1)S(1)}, u32[]{:S(2)}, u32[]{:S(2)}) async-start(bf16[32,1,64,128]{3,2,1,0:T(8,128)(2,1)} %copy.55), calls=%async_computation.3 | async-start | bytes 1048576 | tf_op jit(solution)/shard_map/all_to_all | solution.py:63
  125.8 95.9 %all-reduce.6.cloned.1.call-start = ((), (), s32[]{:S(2)}) async-start(), calls=%async_computation.4 | async-start | bytes 393216 | tf_op jit(solution)/shard_map/psum | solution.py:152
  129.8 93.6 %copy-start.13 = (bf16[64,64]{1,0:T(8,128)(2,1)S(1)}, bf16[64,64]{1,0:T(8,128)(2,1)}, u32[]{:S(2)}) copy-start(bf16[64,64]{1,0:T(8,128)(2,1)} %param.17) | copy-start | bytes 24580
Sparse Core Ops, SparseCore 0:
  130.6 91.0 all-reduce.5
where the time goes:
time: 242 us; the launch traced here: 241 us
  waiting for transfers between devices  102 us (42%)
  between operations  48.2 us (20%)
  matrix products  43.7 us (18%)
  starting transfers between devices  33.4 us (14%)
  local copies, waits for them, and re-layouts  8.26 us (3%)
  other arithmetic  5.98 us (2%)
    psum x1, waiting for transfers between devices, per_device(): summed = lax.psum(local_grad, 'gx')  89 us
    all_to_all x2, starting transfers between devices, spectral(): lax.all_to_all(slab, 'gx', split_axis=1, concat_axis=0, tiled=True)  16.4 us
    dot_general x6, matrix products, per_device(): jnp.einsum('oc,xycz->xyoz', kernel_weight[tile], moved, preferred_element...  10.4 us
    all_to_all x2, starting transfers between devices, spectral(): return lax.all_to_all(result, 'gx', split_axis=0, concat_axis=1, tiled=True)  10.1 us
    dot_general x6, matrix products, per_device(): jnp.einsum('oc,xyoz->xycz', kernel_weight[tile], back_moved, preferred_el...  9.73 us
    all_to_all x2, waiting for transfers between devices, spectral(): return lax.all_to_all(result, 'gx', split_axis=0, concat_axis=1, tiled=True)  7.95 us
    dot_general x1, matrix products, per_device(): jnp.einsum('oc,xyoz->xycz', lap_weight, laplace_ext(ext_grad), preferred_...  7.47 us
    dot_general x6, matrix products, per_device(): jnp.einsum('xyoz,xycz->oc', back_moved, features, preferred_element_type=...  6.05 us
  transfers between devices with their start and end apart: 9, of which 3 were waited for; matrix products, arithmetic and copies ran while one was open for 14% of the time, Pallas kernels for 0%

commit v1 on v0

--- a/solution.py
+++ b/solution.py
@@ -149,7 +149,7 @@
     scaling = float(
         lax.axis_size("gx") * features.shape[0] * features.shape[1] * features.shape[3]
     ) ** (-0.5)
-    summed = lax.psum(local_grad, "gx")
+    summed = jnp.sum(lax.all_gather(local_grad, "gx"), axis=0)
     return (input_grad.astype(jnp.bfloat16), summed * scaling)
 
 

time: 242 us -> 167 us (0.69)
  waiting for transfers between devices: 102 us -> 30 us
  matrix products: 43.7 us -> 37.8 us
    psum x1 -> x0, waiting for transfers between devices: 89 us -> none  [per_device(): summed = lax.psum(local_grad, 'gx')]
    all_to_all x2, waiting for transfers between devices: 7.95 us -> 15.4 us  [spectral(): return lax.all_to_all(result, 'gx', split_axis=0, concat_axis=1, tiled=True)]
    all_gather x0 -> x1, waiting for transfers between devices: none -> 6.79 us  [per_device(): summed = jnp.sum(lax.all_gather(local_grad, 'gx'), axis=0)]
    dot_general x6, matrix products: 6.05 us -> 2.36 us  [per_device(): jnp.einsum('xyoz,xycz->oc', back_moved, features, preferred_element_type=...]
    all_to_all x2, waiting for transfers between devices: 4.71 us -> 7.82 us  [spectral(): lax.all_to_all(slab, 'gx', split_axis=1, concat_axis=0, tiled=True)]
  transfers between devices with their start and end apart: 9 -> 9, of which waited for: 3 -> 4; matrix products, arithmetic and copies ran while one was open for 14% -> 25% of each run, Pallas kernels for 0% -> 0%
where the time goes in v1:
time: 167 us; the launch traced here: 166 us
  between operations  48.6 us (29%)
  matrix products  37.8 us (23%)
  starting transfers between devices  33.6 us (20%)
  waiting for transfers between devices  30 us (18%)
  local copies, waits for them, and re-layouts  8.37 us (5%)
  other arithmetic  7.79 us (5%)
    all_to_all x2, starting transfers between devices, spectral(): lax.all_to_all(slab, 'gx', split_axis=1, concat_axis=0, tiled=True)  16.3 us
    all_to_all x2, waiting for transfers between devices, spectral(): return lax.all_to_all(result, 'gx', split_axis=0, concat_axis=1, tiled=True)  15.4 us
    dot_general x6, matrix products, per_device(): jnp.einsum('oc,xycz->xyoz', kernel_weight[tile], moved, preferred_element...  10.4 us
    all_to_all x2, starting transfers between devices, spectral(): return lax.all_to_all(result, 'gx', split_axis=0, concat_axis=1, tiled=True)  10.1 us
    all_to_all x2, waiting for transfers between devices, spectral(): lax.all_to_all(slab, 'gx', split_axis=1, concat_axis=0, tiled=True)  7.82 us
    dot_general x1, matrix products, per_device(): jnp.einsum('oc,xyoz->xycz', lap_weight, laplace_ext(ext_grad), preferred_...  7.58 us
    dot_general x6, matrix products, per_device(): jnp.einsum('oc,xyoz->xycz', kernel_weight[tile], back_moved, preferred_el...  7.52 us
    all_gather x1, waiting for transfers between devices, per_device(): summed = jnp.sum(lax.all_gather(local_grad, 'gx'), axis=0)  6.79 us
  transfers between devices with their start and end apart: 9, of which 4 were waited for; matrix products, arithmetic and copies ran while one was open for 25% of the time, Pallas kernels for 0%

profile of v1, /device:TPU:0, one launch (start us, length us, event | category | flops | bytes accessed | tf_op | source)
XLA Modules:
  0.0 166.1 jit_solution(18212611988768496173)
XLA Ops:
  7.2 1.1 fusion.148
  8.4 2.4 %collective-permute-start = (bf16[1,16,64,128]{3,2,1,0:T(8,128)(2,1)S(1)}, bf16[1,16,64,128]{3,2,1,0:T(8,128)(2,1)S(1)}, u32[]{:S(2)}, u32[]{:S(2)}) collective-permute-start(bf16[1,16,64,128]{3,2,1,0:T(8,128)(2,1)S(1)} %get-tuple-element.5), channel_id=1, source_target_pairs={{0,1},{1,2},{2,3},{3,4},{4,5},{5,6},{6,7},{7,8},{8,9},{9,10},{10,1... | collective-permute-start | bytes 786440 | tf_op jit(solution)/shard_map/ppermute | solution.py:19
  10.7 1.3 collective-permute-start.1
  12.0 1.9 %copy.40 = bf16[2,16,64,128]{3,2,0,1:T(8,128)(2,1)} copy(bf16[2,16,64,128]{3,2,1,0:T(8,128)(2,1)} %param.10) | data formatting | bytes 1048576 | tf_op args[0]
  13.9 9.4 %all-to-all-start = ((bf16[2,16,64,128]{3,2,0,1:T(8,128)(2,1)}), bf16[2,16,64,128]{3,2,0,1:T(8,128)(2,1)S(1)}, u32[]{:S(2)}, u32[]{:S(2)}) async-start(bf16[2,16,64,128]{3,2,0,1:T(8,128)(2,1)} %copy.40), calls=%async_computation | async-start | bytes 1048576 | tf_op jit(solution)/shard_map/all_to_all | solution.py:58
  23.4 1.3 fusion.76
  49.7 1.5 fusion.48
  51.2 1.4 fusion.49
  52.6 1.1 convolution_convert_fusion.4
  56.0 6.0 %all-to-all-start.1 = ((bf16[32,1,64,128]{3,2,1,0:T(8,128)(2,1)}), bf16[32,1,64,128]{3,2,1,0:T(8,128)(2,1)S(1)}, u32[]{:S(2)}, u32[]{:S(2)}) async-start(bf16[32,1,64,128]{3,2,1,0:T(8,128)(2,1)} %copy.44), calls=%async_computation.1 | async-start | bytes 1048576 | tf_op jit(solution)/shard_map/all_to_all | solution.py:63
  62.8 1.4 fusion.50
  64.2 1.4 fusion.51
  65.6 2.8 %convolution_add_fusion.1 = f32[2,16,128,64]{2,3,1,0:T(8,128)} fusion(f32[2,16,128,64]{2,3,1,0:T(8,128)S(1)} %copy-done.7, f32[4,18,64,130]{3,2,1,0:T(8,128)S(1)} %pad_convert_fusion.1, bf16[64,64]{1,0:T(8,128)(2,1)S(1)} %copy-done.17), kind=kOutput, calls=%fused_computation.37 | convolution fusion | flops 35913728 | bytes 9453568 | tf_op jit(solution)/shard_map/oc,xycz->xyoz/dot_general | solution.py:117
  68.5 8.0 %all-to-all-done.1 = bf16[32,1,64,128]{3,2,1,0:T(8,128)(2,1)S(1)} async-done(((bf16[32,1,64,128]{3,2,1,0:T(8,128)(2,1)}), bf16[32,1,64,128]{3,2,1,0:T(8,128)(2,1)S(1)}, u32[]{:S(2)}, u32[]{:S(2)}) %all-to-all-start.1) | async-done | bytes 524320 | tf_op jit(solution)/shard_map/all_to_all | solution.py:63
  77.2 4.2 %fusion.33 = bf16[2,16,64,128]{3,2,1,0:T(8,128)(2,1)S(1)} fusion(bf16[2,16,64,128]{3,2,1,0:T(8,128)(2,1)} %param.11, f32[2,16,128,64]{2,3,1,0:T(8,128)} %fusion.51, f32[2,16,128,64]{2,3,1,0:T(8,128)} %fusion.50, f32[2,16,128,64]{2,3,1,0:T(8,128)} %fusion.49, f32[2,16,128,64]{2,3,1,0:T(8,128)} %fusion.48, f32[2,16,128,64]{2,3,1,0:T(8,128)S(1)} %fusion.47, ...), kind=kOutput, calls=%fused_computation.72 | convolution fusion | flops 41680896 | bytes 8946188 | tf_op jit(solution)/shard_map/oc,xycz->xyoz/dot_general | solution.py:122
  81.5 1.9 %collective-permute-start.2 = (bf16[1,16,64,128]{3,2,1,0:T(8,128)(2,1)S(1)}, bf16[1,16,64,128]{3,2,1,0:T(8,128)(2,1)S(1)}, u32[]{:S(2)}, u32[]{:S(2)}) collective-permute-start(bf16[1,16,64,128]{3,2,1,0:T(8,128)(2,1)S(1)} %get-tuple-element.2), channel_id=1, source_target_pairs={{0,1},{1,2},{2,3},{3,4},{4,5},{5,6},{6,7},{7,8},{8,9},{9,10},{10,1... | collective-permute-start | bytes 786440 | tf_op jit(solution)/shard_map/ppermute | solution.py:19
  83.4 1.3 collective-permute-start.3
  97.1 6.9 %all-to-all-start.2 = ((bf16[2,16,64,128]{3,2,0,1:T(8,128)(2,1)}), bf16[2,16,64,128]{3,2,0,1:T(8,128)(2,1)}, u32[]{:S(2)}, u32[]{:S(2)}) async-start(bf16[2,16,64,128]{3,2,0,1:T(8,128)(2,1)} %copy.49), calls=%async_computation.2 | async-start | bytes 1048576 | tf_op jit(solution)/shard_map/all_to_all | solution.py:58
  107.6 1.3 fusion.74
  109.3 1.5 convolution_bitcast_fusion.2
  110.8 7.8 %all-to-all-done.2 = bf16[2,16,64,128]{3,2,0,1:T(8,128)(2,1)} async-done(((bf16[2,16,64,128]{3,2,0,1:T(8,128)(2,1)}), bf16[2,16,64,128]{3,2,0,1:T(8,128)(2,1)}, u32[]{:S(2)}, u32[]{:S(2)}) %all-to-all-start.2) | async-done | bytes 524320 | tf_op jit(solution)/shard_map/all_to_all | solution.py:58
  118.6 1.5 fusion.22
  121.9 4.1 %all-to-all-start.3 = ((bf16[32,1,64,128]{3,2,1,0:T(8,128)(2,1)}), bf16[32,1,64,128]{3,2,1,0:T(8,128)(2,1)S(1)}, u32[]{:S(2)}, u32[]{:S(2)}) async-start(bf16[32,1,64,128]{3,2,1,0:T(8,128)(2,1)} %copy.55), calls=%async_computation.3 | async-start | bytes 1048576 | tf_op jit(solution)/shard_map/all_to_all | solution.py:63
  126.0 2.9 %pad_convert_fusion = f32[4,18,64,130]{3,2,1,0:T(8,128)} fusion(bf16[4,16,64,128]{3,2,1,0:T(8,128)(2,1)S(1)} %pad_maximum_fusion), kind=kLoop, calls=%fused_computation.12 | loop fusion | flops 599040 | bytes 3444736 | tf_op jit(solution)/shard_map/convert_element_type | solution.py:67
  128.9 1.4 convolution_bitcast_fusion.3
  130.3 1.5 convolution_bitcast_fusion.4
  131.7 1.4 convolution_bitcast_fusion
  133.1 7.4 %all-to-all-done.3 = bf16[32,1,64,128]{3,2,1,0:T(8,128)(2,1)S(1)} async-done(((bf16[32,1,64,128]{3,2,1,0:T(8,128)(2,1)}), bf16[32,1,64,128]{3,2,1,0:T(8,128)(2,1)S(1)}, u32[]{:S(2)}, u32[]{:S(2)}) %all-to-all-start.3) | async-done | bytes 524320 | tf_op jit(solution)/shard_map/all_to_all | solution.py:63
  140.6 7.6 %fusion.15 = f32[2,16,64,128]{3,2,1,0:T(8,128)S(1)} fusion(f32[2,16,128,64]{2,3,1,0:T(8,128)} %fusion.74, f32[4,18,64,130]{3,2,1,0:T(8,128)} %pad_convert_fusion, bf16[64,64]{1,0:T(8,128)(2,1)S(1)} %copy-done.18, bf16[16,2,1,64,128]{4,3,1,0,2:T(8,128)(2,1)S(1)} %bitcast.308), kind=kOutput, calls=%fused_computation.40 | convolution fusion | flops 36438016 | bytes 9969664 | tf_op jit(solution)/shard_map/oc,xyoz->xycz/dot_general | solution.py:135
  148.2 1.4 fusion.16
  149.6 6.8 %all-gather.3.cloned.1.call-done = f32[96,64,64]{2,1,0:T(8,128)} async-done(((f32[6,64,64]{2,1,0:T(8,128)}), f32[96,64,64]{2,1,0:T(8,128)}) %all-gather.3.cloned.1.call-update) | async-done | bytes 1572880 | tf_op jit(solution)/shard_map/all_gather | solution.py:152
  156.3 2.3 %reduce_sum.9 = f32[6,64,64]{2,1,0:T(8,128)S(1)} reduce(f32[16,6,64,64]{3,2,1,0:T(8,128)} %bitcast.305, f32[]{:T(128)} %constant.158.clone.1), dimensions={0}, to_apply=%region_0.1 | reduce | flops 368640 | bytes 1671172 | tf_op jit(solution)/shard_map/reduce_sum | solution.py:152
  (73 shorter events, 13.5 us)
Async XLA Ops:
  7.2 46.5 %copy-start = (bf16[16,64,64]{2,1,0:T(8,128)(2,1)S(1)}, bf16[16,64,64]{2,1,0:T(8,128)(2,1)}, u32[]{:S(2)}) copy-start(bf16[16,64,64]{2,1,0:T(8,128)(2,1)} %param.18) | copy-start | bytes 393220
  7.2 16.2 %copy-start.1 = (bf16[2,16,64,128]{3,2,1,0:T(8,128)(2,1)S(1)}, bf16[2,16,64,128]{3,2,1,0:T(8,128)(2,1)}, u32[]{:S(2)}) copy-start(bf16[2,16,64,128]{3,2,1,0:T(8,128)(2,1)} %param.10) | copy-start | bytes 1572868
  7.2 16.2 %copy-start.16 = (s32[64]{0:T(128)S(1)}, s32[64]{0:T(128)}, u32[]{:S(2)}) copy-start(s32[64]{0:T(128)} %param.13) | copy-start | bytes 772
  7.2 16.2 %copy-start.10 = (bf16[64,64]{1,0:T(8,128)(2,1)S(1)}, bf16[64,64]{1,0:T(8,128)(2,1)}, u32[]{:S(2)}) copy-start(bf16[64,64]{1,0:T(8,128)(2,1)} %param.15) | copy-start | bytes 24580
  7.2 17.4 %copy-start.12 = (s32[2,16,128]{2,1,0:T(8,128)S(1)}, s32[2,16,128]{2,1,0:T(8,128)}, u32[]{:S(2)}) copy-start(s32[2,16,128]{2,1,0:T(8,128)} %param.12) | copy-start | bytes 49156
  7.2 18.0 %copy-start.11 = (s32[6,3]{0,1:T(4,128)S(1)}, s32[6,3]{0,1:T(4,128)}, u32[]{:S(2)}) copy-start(s32[6,3]{0,1:T(4,128)} %param.14) | copy-start | bytes 220
  8.4 40.7 %collective-permute-start = (bf16[1,16,64,128]{3,2,1,0:T(8,128)(2,1)S(1)}, bf16[1,16,64,128]{3,2,1,0:T(8,128)(2,1)S(1)}, u32[]{:S(2)}, u32[]{:S(2)}) collective-permute-start(bf16[1,16,64,128]{3,2,1,0:T(8,128)(2,1)S(1)} %get-tuple-element.5), channel_id=1, source_target_pairs={{0,1},{1,2},{2,3},{3,4},{4,5},{5,6},{6,7},{7,8},{8,9},{9,10},{10,1... | collective-permute-start | bytes 786440 | tf_op jit(solution)/shard_map/ppermute | solution.py:19
  10.7 38.4 %collective-permute-start.1 = (bf16[1,16,64,128]{3,2,1,0:T(8,128)(2,1)S(1)}, bf16[1,16,64,128]{3,2,1,0:T(8,128)(2,1)S(1)}, u32[]{:S(2)}, u32[]{:S(2)}) collective-permute-start(bf16[1,16,64,128]{3,2,1,0:T(8,128)(2,1)S(1)} %get-tuple-element.4), channel_id=1, source_target_pairs={{1,0},{2,1},{3,2},{4,3},{5,4},{6,5},{7,6},{8,7},{9,8},{10,9},{11,1... | collective-permute-start | bytes 786440 | tf_op jit(solution)/shard_map/ppermute | solution.py:21
  13.9 35.3 %copy-start.8 = (bf16[6,64,64]{2,1,0:T(8,128)(2,1)S(1)}, bf16[6,64,64]{2,1,0:T(8,128)(2,1)}, u32[]{:S(2)}) copy-start(bf16[6,64,64]{2,1,0:T(8,128)(2,1)} %param.16) | copy-start | bytes 147460
  13.9 38.7 %all-to-all-start = ((bf16[2,16,64,128]{3,2,0,1:T(8,128)(2,1)}), bf16[2,16,64,128]{3,2,0,1:T(8,128)(2,1)S(1)}, u32[]{:S(2)}, u32[]{:S(2)}) async-start(bf16[2,16,64,128]{3,2,0,1:T(8,128)(2,1)} %copy.40), calls=%async_computation | async-start | bytes 1048576 | tf_op jit(solution)/shard_map/all_to_all | solution.py:58
  56.0 20.5 %all-to-all-start.1 = ((bf16[32,1,64,128]{3,2,1,0:T(8,128)(2,1)}), bf16[32,1,64,128]{3,2,1,0:T(8,128)(2,1)S(1)}, u32[]{:S(2)}, u32[]{:S(2)}) async-start(bf16[32,1,64,128]{3,2,1,0:T(8,128)(2,1)} %copy.44), calls=%async_computation.1 | async-start | bytes 1048576 | tf_op jit(solution)/shard_map/all_to_all | solution.py:63
  62.8 2.9 %copy-start.7 = (f32[2,16,128,64]{2,3,1,0:T(8,128)S(1)}, f32[2,16,128,64]{2,3,1,0:T(8,128)}, u32[]{:S(2)}) copy-start(f32[2,16,128,64]{2,3,1,0:T(8,128)} %fusion.76) | copy-start | bytes 3145732
  62.8 2.9 %copy-start.17 = (bf16[64,64]{1,0:T(8,128)(2,1)S(1)}, bf16[64,64]{1,0:T(8,128)(2,1)}, u32[]{:S(2)}) copy-start(bf16[64,64]{1,0:T(8,128)(2,1)} %param.17) | copy-start | bytes 24580
  64.2 13.0 %copy-start.15 = (f32[64]{0:T(128)S(1)}, f32[64]{0:T(128)}, u32[]{:S(2)}) copy-start(f32[64]{0:T(128)} %param.19) | copy-start | bytes 772
  76.4 0.8 copy-start.6
  81.5 22.8 %collective-permute-start.2 = (bf16[1,16,64,128]{3,2,1,0:T(8,128)(2,1)S(1)}, bf16[1,16,64,128]{3,2,1,0:T(8,128)(2,1)S(1)}, u32[]{:S(2)}, u32[]{:S(2)}) collective-permute-start(bf16[1,16,64,128]{3,2,1,0:T(8,128)(2,1)S(1)} %get-tuple-element.2), channel_id=1, source_target_pairs={{0,1},{1,2},{2,3},{3,4},{4,5},{5,6},{6,7},{7,8},{8,9},{9,10},{10,1... | collective-permute-start | bytes 786440 | tf_op jit(solution)/shard_map/ppermute | solution.py:19
  83.4 20.9 %collective-permute-start.3 = (bf16[1,16,64,128]{3,2,1,0:T(8,128)(2,1)S(1)}, bf16[1,16,64,128]{3,2,1,0:T(8,128)(2,1)S(1)}, u32[]{:S(2)}, u32[]{:S(2)}) collective-permute-start(bf16[1,16,64,128]{3,2,1,0:T(8,128)(2,1)S(1)} %get-tuple-element.3), channel_id=1, source_target_pairs={{1,0},{2,1},{3,2},{4,3},{5,4},{6,5},{7,6},{8,7},{9,8},{10,9},{11,1... | collective-permute-start | bytes 786440 | tf_op jit(solution)/shard_map/ppermute | solution.py:21
  97.1 21.5 %all-to-all-start.2 = ((bf16[2,16,64,128]{3,2,0,1:T(8,128)(2,1)}), bf16[2,16,64,128]{3,2,0,1:T(8,128)(2,1)}, u32[]{:S(2)}, u32[]{:S(2)}) async-start(bf16[2,16,64,128]{3,2,0,1:T(8,128)(2,1)} %copy.49), calls=%async_computation.2 | async-start | bytes 1048576 | tf_op jit(solution)/shard_map/all_to_all | solution.py:58
  104.1 52.3 %all-gather.3.cloned.1.call-start = ((), (), s32[]{:S(2)}) async-start(), calls=%async_computation.4 | async-start | bytes 3342336 | tf_op jit(solution)/shard_map/all_gather | solution.py:152
  106.9 0.7 copy-start.9
  107.6 11.0 %copy-start.13 = (f32[16]{0:T(128)S(1)}, f32[16]{0:T(128)}, u32[]{:S(2)}) copy-start(f32[16]{0:T(128)} %get-tuple-element.27) | copy-start | bytes 196
  107.6 11.0 %copy-start.14 = (f32[32]{0:T(128)S(1)}, f32[32]{0:T(128)}, u32[]{:S(2)}) copy-start(f32[32]{0:T(128)} %multiply_add_fusion) | copy-start | bytes 388
  121.9 18.7 %all-to-all-start.3 = ((bf16[32,1,64,128]{3,2,1,0:T(8,128)(2,1)}), bf16[32,1,64,128]{3,2,1,0:T(8,128)(2,1)S(1)}, u32[]{:S(2)}, u32[]{:S(2)}) async-start(bf16[32,1,64,128]{3,2,1,0:T(8,128)(2,1)} %copy.55), calls=%async_computation.3 | async-start | bytes 1048576 | tf_op jit(solution)/shard_map/all_to_all | solution.py:63
  130.3 10.3 %copy-start.18 = (bf16[64,64]{1,0:T(8,128)(2,1)S(1)}, bf16[64,64]{1,0:T(8,128)(2,1)}, u32[]{:S(2)}) copy-start(bf16[64,64]{1,0:T(8,128)(2,1)} %param.17) | copy-start | bytes 24580
  140.5 7.6 %copy-start.2 = (f32[2,16,64,128]{3,2,1,0:T(8,128)S(1)}, f32[2,16,64,128]{3,2,1,0:T(8,128)}, u32[]{:S(2)}) copy-start(f32[2,16,64,128]{3,2,1,0:T(8,128)} %convolution_bitcast_fusion.2) | copy-start | bytes 3145732
  140.5 7.6 %copy-start.3 = (f32[2,16,64,128]{3,2,1,0:T(8,128)S(1)}, f32[2,16,64,128]{3,2,1,0:T(8,128)}, u32[]{:S(2)}) copy-start(f32[2,16,64,128]{3,2,1,0:T(8,128)} %convolution_bitcast_fusion.3) | copy-start | bytes 3145732
  140.5 7.6 %copy-start.4 = (f32[2,16,64,128]{3,2,1,0:T(8,128)S(1)}, f32[2,16,64,128]{3,2,1,0:T(8,128)}, u32[]{:S(2)}) copy-start(f32[2,16,64,128]{3,2,1,0:T(8,128)} %convolution_bitcast_fusion.4) | copy-start | bytes 3145732
  140.5 7.6 %copy-start.5 = (f32[2,16,64,128]{3,2,1,0:T(8,128)S(1)}, f32[2,16,64,128]{3,2,1,0:T(8,128)}, u32[]{:S(2)}) copy-start(f32[2,16,64,128]{3,2,1,0:T(8,128)} %convolution_bitcast_fusion) | copy-start | bytes 3145732
Sparse Core Ops, SparseCore 0:
  107.8 48.5 all-gather.2
